TPU v7x, 32 devices: a whole 2x2x4 slice. The times are simulated.
32 devices in a mesh: ctx: 8 (over y, x, core), tp: 4 (over z).
Axes of the slice: x: 2, y: 2, z: 4, core: 2. Of those that a mesh axis runs over, the one named last changes fastest.
Arguments:
- query_mr: bfloat16 [2048, 8192], P('ctx', 'tp'), may hold values from -6 to 6
- key_mr: bfloat16 [2048, 8192], P('ctx', 'tp'), may hold values from -6 to 6
- value_mr: bfloat16 [2048, 8192], P('ctx', 'tp'), may hold values from -6 to 6
- query_li: bfloat16 [2048, 8192], P('ctx', 'tp'), may hold values from -6 to 6
- key_li: bfloat16 [2048, 8192], P('ctx', 'tp'), may hold values from -6 to 6
- cotangent: bfloat16 [2048, 8192], P('ctx', 'tp'), may hold values from -6 to 6
- mr_taps: float32 [128, 8192], P(None, 'tp'), may hold values from -0.5 to 0.5
- decay_rates: float32 [8], replicated, may hold values from 4.8828126e-05 to 0.03
- residues: float32 [8, 8192], P(None, 'tp'), may hold values from -2 to 2
Outputs:
- grad_query_mr: bfloat16 [2048, 8192], P('ctx', 'tp')
- grad_key_mr: bfloat16 [2048, 8192], P('ctx', 'tp')
- grad_value_mr: bfloat16 [2048, 8192], P('ctx', 'tp')
- grad_query_li: bfloat16 [2048, 8192], P('ctx', 'tp')
- grad_key_li: bfloat16 [2048, 8192], P('ctx', 'tp')
- grad_taps: float32 [128, 8192], P(None, 'tp')
- grad_residues: float32 [8, 8192], P(None, 'tp')
All inputs are finite; a program needn't handle non-finite values.
Results may differ from a plain program's by a relative error of at most 0.001.
Values may be sent and summed in bfloat16 or wider, within the bound.
A program may use at most 128 MiB of HBM per device.

v0:
```python
import math
import jax
import jax.numpy as jnp
from jax import lax
from jax.sharding import PartitionSpec as P

BLOCK = 128
highest = lax.Precision.HIGHEST


def from_behind(value, axis, by):
    size = lax.axis_size(axis)
    pairs = [(i, i + by) for i in range(size) if 0 <= i + by < size]
    return lax.ppermute(value, axis, pairs)


def depthwise(signal, kernel):
    channels = signal.shape[1]
    output = lax.conv_general_dilated(
        signal[None],
        kernel[:, None, :],
        (1,),
        "VALID",
        dimension_numbers=("NWC", "WIO", "NWC"),
        feature_group_count=channels,
        precision=highest,
    )
    return output[0]


def linked(earlier, later):
    return (earlier[0] * later[1] + later[0], earlier[1] * later[1])


def modal_terms(inputs, cotangents, decay_rates, residues, block_len):
    length, channels = inputs.shape
    blocks = length // block_len
    in_blocks = inputs.reshape(blocks, block_len, channels)
    co_blocks = cotangents.reshape(blocks, block_len, channels)
    places = jnp.arange(block_len, dtype=jnp.float32)
    offsets = places[:, None] - places[None, :]
    modes = decay_rates.shape[0]

    def one_mode(mode, state):
        conv_sum, back_sum, residue_grad, end_rows, start_rows = state
        decay_rate = decay_rates[mode]
        residue_row = lax.dynamic_index_in_dim(residues, mode, 0, keepdims=False)
        mode_scale = jnp.sqrt(-jnp.expm1(-2.0 * decay_rate))
        toeplitz = jnp.where(
            offsets >= 0.0, mode_scale * jnp.exp(-decay_rate * jnp.maximum(offsets, 0.0)), 0.0
        )
        block_pows = jnp.full((blocks, 1), jnp.exp(-decay_rate * block_len), jnp.float32)
        forward = jnp.einsum("tj,bjc->btc", toeplitz, in_blocks, precision=highest)
        backward = jnp.einsum("jt,bjc->btc", toeplitz, co_blocks, precision=highest)
        forward_incl = lax.associative_scan(linked, (forward[:, -1], block_pows))[0]
        backward_incl = lax.associative_scan(linked, (backward[:, 0], block_pows), reverse=True)[0]
        zero_row = jnp.zeros((1, channels), jnp.float32)
        forward_in = jnp.concatenate([zero_row, forward_incl[:-1]], 0)
        backward_in = jnp.concatenate([backward_incl[1:], zero_row], 0)
        lead_pows = jnp.exp(-decay_rate * (places + 1.0))
        tail_pows = jnp.exp(-decay_rate * (block_len - places))
        states = (forward + lead_pows[None, :, None] * forward_in[:, None, :]).reshape(
            length, channels
        )
        reverse_states = (backward + tail_pows[None, :, None] * backward_in[:, None, :]).reshape(
            length, channels
        )
        conv_sum = conv_sum + residue_row[None, :] * states
        back_sum = back_sum + residue_row[None, :] * reverse_states
        residue_grad = lax.dynamic_update_index_in_dim(
            residue_grad, jnp.sum(inputs * reverse_states, 0), mode, 0
        )
        end_rows = lax.dynamic_update_index_in_dim(end_rows, states[length - 1], mode, 0)
        start_rows = lax.dynamic_update_index_in_dim(start_rows, reverse_states[0], mode, 0)
        return (conv_sum, back_sum, residue_grad, end_rows, start_rows)

    zero_field = jnp.zeros((length, channels), jnp.float32)
    zero_modes = jnp.zeros((modes, channels), jnp.float32)
    return lax.fori_loop(
        0, modes, one_mode, (zero_field, zero_field, zero_modes, zero_modes, zero_modes)
    )


def per_device(
    query_mr, key_mr, value_mr, query_li, key_li, cotangent, mr_taps, decay_rates, residues
):
    length, channels = query_mr.shape
    taps_len = mr_taps.shape[0]
    rim_rows = taps_len - 1
    devices_ctx = lax.axis_size("ctx")
    seq_len = length * devices_ctx
    prior_key, prior_value = from_behind(
        (key_mr[length - rim_rows :], value_mr[length - rim_rows :]), "ctx", 1
    )
    key_first = key_mr.astype(jnp.float32)
    value_first = value_mr.astype(jnp.float32)
    query_first = query_mr.astype(jnp.float32)
    mixed_in = jnp.concatenate([prior_key, key_mr], 0).astype(jnp.float32) * jnp.concatenate(
        [prior_value, value_mr], 0
    ).astype(jnp.float32)
    mr_conv = depthwise(mixed_in, mr_taps[::-1])
    mr_out = query_first * mr_conv
    key_second = key_li.astype(jnp.float32)
    cotan = cotangent.astype(jnp.float32)
    li_input = key_second * mr_out
    li_cotan = cotan * query_li.astype(jnp.float32)
    regrouped = lax.all_to_all(
        jnp.stack([li_input, li_cotan]), "ctx", split_axis=2, concat_axis=1, tiled=True
    )
    piece_cols = channels // devices_ctx
    local_residues = lax.dynamic_slice_in_dim(
        residues, lax.axis_index("ctx") * piece_cols, piece_cols, 1
    )
    conv_seq, back_seq, residue_piece, unused_ends, unused_starts = modal_terms(
        regrouped[0], regrouped[1], decay_rates, local_residues, BLOCK
    )
    returned = lax.all_to_all(
        jnp.stack([conv_seq, back_seq]), "ctx", split_axis=1, concat_axis=2, tiled=True
    )
    li_conv = returned[0]
    li_back = returned[1]
    residue_sum = lax.all_gather(residue_piece, "ctx", axis=1, tiled=True)
    grad_query_li = (cotan * li_conv).astype(jnp.bfloat16)
    grad_key_li = (mr_out * li_back).astype(jnp.bfloat16)
    mr_grad = cotan + key_second * li_back
    grad_query_mr = (mr_grad * mr_conv).astype(jnp.bfloat16)
    mr_cotan = mr_grad * query_first
    next_rows = from_behind(mr_cotan[:rim_rows], "ctx", -1)
    mixed_grad = depthwise(jnp.concatenate([mr_cotan, next_rows], 0), mr_taps)
    grad_key_mr = (mixed_grad * value_first).astype(jnp.bfloat16)
    grad_value_mr = (mixed_grad * key_first).astype(jnp.bfloat16)
    tap_part = depthwise(mixed_in, mr_cotan)[::-1]
    tap_sum = lax.psum(tap_part, "ctx")
    factor = 1.0 / math.sqrt(seq_len)
    return (
        grad_query_mr,
        grad_key_mr,
        grad_value_mr,
        grad_query_li,
        grad_key_li,
        tap_sum * factor,
        residue_sum * factor,
    )


def solution(mesh):
    placed = (
        P("ctx", "tp"),
        P("ctx", "tp"),
        P("ctx", "tp"),
        P("ctx", "tp"),
        P("ctx", "tp"),
        P("ctx", "tp"),
        P(None, "tp"),
        P(),
        P(None, "tp"),
    )
    return jax.shard_map(
        per_device,
        mesh=mesh,
        in_specs=placed,
        out_specs=(
            P("ctx", "tp"),
            P("ctx", "tp"),
            P("ctx", "tp"),
            P("ctx", "tp"),
            P("ctx", "tp"),
            P(None, "tp"),
            P(None, "tp"),
        ),
        check_vma=False,
    )
```

profile of v0, /device:TPU:0, one launch (start us, length us, event | category | flops | bytes accessed | tf_op | source)
XLA Modules:
  0.0 570.9 jit_solution(17721856543120809470)
XLA Ops:
  13.7 5.3 collective-permute-start.1
  19.0 8.9 %rev.15 = f32[128,2048]{1,0:T(8,128)} reverse(f32[128,2048]{1,0:T(8,128)} %param.17), dimensions={0} | reverse | bytes 2097152 | tf_op jit(solution)/shard_map/rev | solution.py:101
  31.3 21.5 %fusion.49 = f32[1,256,2048]{2,0,1:T(1,128)S(1)} fusion(f32[1,383,2048]{2,1,0:T(8,128)S(1)} %convert_multiply_fusion, f32[128,1,2048]{2,0,1:T(8,128)S(1)} %bitcast.140), kind=kOutput, calls=%fused_computation.100 | convolution fusion | flops 805306368 | bytes 6283264 | tf_op jit(solution)/shard_map/conv_general_dilated | solution.py:19
  56.9 7.3 %copy.48 = f32[2,256,2048]{1,0,2:T(2,128)} copy(f32[2,256,2048]{2,1,0:T(8,128)} %pad_maximum_fusion.6) | data formatting | bytes 8388608 | tf_op jit(solution)/shard_map/stack | solution.py:108
  64.1 4.6 all-to-all-start
  68.8 49.0 %all-to-all-done = f32[2,256,2048]{1,0,2:T(2,128)} async-done(((f32[2,256,2048]{1,0,2:T(2,128)}), f32[2,256,2048]{1,0,2:T(2,128)}, u32[]{:S(2)}, u32[]{:S(2)}) %all-to-all-start) | async-done | bytes 4194336 | tf_op jit(solution)/shard_map/all_to_all | solution.py:107
  117.8 9.6 %fusion.58 = (f32[1,8,256,256]{2,0,3,1:T(1,128)}, f32[1,8,256,256]{2,0,3,1:T(1,128)}) fusion(f32[2,8,256,256]{2,0,3,1:T(2,128)} %bitcast.8), kind=kLoop, calls=%fused_computation.113 | loop fusion | bytes 8388608 | tf_op jit(solution)/shard_map/slice | solution.py:115
  127.4 4.5 copy.49
  131.9 6.0 %copy.50 = f32[1,8,256,256]{3,2,1,0:T(8,128)} copy(f32[1,8,256,256]{2,0,3,1:T(1,128)} %get-tuple-element.304) | data formatting | bytes 4194304 | tf_op jit(solution)/shard_map/slice | solution.py:115
  138.0 240.8 %while.19 = (s32[]{:T(128)}, f32[2048,256]{1,0:T(8,128)}, f32[2048,256]{1,0:T(8,128)}, f32[8,256]{1,0:T(8,128)S(1)}, f32[8,256]{1,0:T(8,128)S(1)}, /*index=5*/f3...) while((s32[]{:T(128)}, f32[2048,256]{1,0:T(8,128)}, ...), condition=%wide.region_2.3_spmd.clone.clone, body=%wide.region_0.2_spmd.clone.clone.sunk | while | flops 1617155328 | bytes 74435056 | solution.py:79
  162.0 4.9 fusion.90
  191.0 6.2 %fusion.90 = (f32[2048,256]{1,0:T(8,128)}, f32[2048,256]{1,0:T(8,128)}) fusion(f32[16,128,256]{2,1,0:T(8,128)} %copy.106, f32[2048,256]{1,0:T(8,128)} %get-tuple-element.414, f32[256]{0:T(256)S(1)} %bitcast.142, pred[]{:T(512)S(6)} %compare.24, f32[16,128,256]{2,1,0:T(8,128)} %multiply_add_fusion.22, f32[2048,256]{1,0:T(8,128)} %get-tuple-element.413), kind=kLoop, calls=%fused_computation.3.clone.1 | loop fusion | flops 3145728 | bytes 12583937 | tf_op jit(solution)/shard_map/while/body/eval_jaxpr/add | solution.py:69
  221.3 6.2 %fusion.90 = (f32[2048,256]{1,0:T(8,128)}, f32[2048,256]{1,0:T(8,128)}) fusion(f32[16,128,256]{2,1,0:T(8,128)} %copy.106, f32[2048,256]{1,0:T(8,128)} %get-tuple-element.414, f32[256]{0:T(256)S(1)} %bitcast.142, pred[]{:T(512)S(6)} %compare.24, f32[16,128,256]{2,1,0:T(8,128)} %multiply_add_fusion.22, f32[2048,256]{1,0:T(8,128)} %get-tuple-element.413), kind=kLoop, calls=%fused_computation.3.clone.1 | loop fusion | flops 3145728 | bytes 12583937 | tf_op jit(solution)/shard_map/while/body/eval_jaxpr/add | solution.py:69
  251.5 6.2 %fusion.90 = (f32[2048,256]{1,0:T(8,128)}, f32[2048,256]{1,0:T(8,128)}) fusion(f32[16,128,256]{2,1,0:T(8,128)} %copy.106, f32[2048,256]{1,0:T(8,128)} %get-tuple-element.414, f32[256]{0:T(256)S(1)} %bitcast.142, pred[]{:T(512)S(6)} %compare.24, f32[16,128,256]{2,1,0:T(8,128)} %multiply_add_fusion.22, f32[2048,256]{1,0:T(8,128)} %get-tuple-element.413), kind=kLoop, calls=%fused_computation.3.clone.1 | loop fusion | flops 3145728 | bytes 12583937 | tf_op jit(solution)/shard_map/while/body/eval_jaxpr/add | solution.py:69
  281.8 6.2 %fusion.90 = (f32[2048,256]{1,0:T(8,128)}, f32[2048,256]{1,0:T(8,128)}) fusion(f32[16,128,256]{2,1,0:T(8,128)} %copy.106, f32[2048,256]{1,0:T(8,128)} %get-tuple-element.414, f32[256]{0:T(256)S(1)} %bitcast.142, pred[]{:T(512)S(6)} %compare.24, f32[16,128,256]{2,1,0:T(8,128)} %multiply_add_fusion.22, f32[2048,256]{1,0:T(8,128)} %get-tuple-element.413), kind=kLoop, calls=%fused_computation.3.clone.1 | loop fusion | flops 3145728 | bytes 12583937 | tf_op jit(solution)/shard_map/while/body/eval_jaxpr/add | solution.py:69
  312.0 6.2 %fusion.90 = (f32[2048,256]{1,0:T(8,128)}, f32[2048,256]{1,0:T(8,128)}) fusion(f32[16,128,256]{2,1,0:T(8,128)} %copy.106, f32[2048,256]{1,0:T(8,128)} %get-tuple-element.414, f32[256]{0:T(256)S(1)} %bitcast.142, pred[]{:T(512)S(6)} %compare.24, f32[16,128,256]{2,1,0:T(8,128)} %multiply_add_fusion.22, f32[2048,256]{1,0:T(8,128)} %get-tuple-element.413), kind=kLoop, calls=%fused_computation.3.clone.1 | loop fusion | flops 3145728 | bytes 12583937 | tf_op jit(solution)/shard_map/while/body/eval_jaxpr/add | solution.py:69
  342.3 6.2 %fusion.90 = (f32[2048,256]{1,0:T(8,128)}, f32[2048,256]{1,0:T(8,128)}) fusion(f32[16,128,256]{2,1,0:T(8,128)} %copy.106, f32[2048,256]{1,0:T(8,128)} %get-tuple-element.414, f32[256]{0:T(256)S(1)} %bitcast.142, pred[]{:T(512)S(6)} %compare.24, f32[16,128,256]{2,1,0:T(8,128)} %multiply_add_fusion.22, f32[2048,256]{1,0:T(8,128)} %get-tuple-element.413), kind=kLoop, calls=%fused_computation.3.clone.1 | loop fusion | flops 3145728 | bytes 12583937 | tf_op jit(solution)/shard_map/while/body/eval_jaxpr/add | solution.py:69
  372.6 6.2 %fusion.90 = (f32[2048,256]{1,0:T(8,128)}, f32[2048,256]{1,0:T(8,128)}) fusion(f32[16,128,256]{2,1,0:T(8,128)} %copy.106, f32[2048,256]{1,0:T(8,128)} %get-tuple-element.414, f32[256]{0:T(256)S(1)} %bitcast.142, pred[]{:T(512)S(6)} %compare.24, f32[16,128,256]{2,1,0:T(8,128)} %multiply_add_fusion.22, f32[2048,256]{1,0:T(8,128)} %get-tuple-element.413), kind=kLoop, calls=%fused_computation.3.clone.1 | loop fusion | flops 3145728 | bytes 12583937 | tf_op jit(solution)/shard_map/while/body/eval_jaxpr/add | solution.py:69
  387.8 51.5 %all_to_all.30 = f32[2,2048,256]{2,0,1:T(2,128)S(1)} all-to-all(f32[2,2048,256]{2,0,1:T(2,128)S(1)} %pad_maximum_fusion.7), channel_id=1, replica_groups=mesh['ctx'=8,'tp'=4] {'ctx'}, dimensions={1} | all-to-all | bytes 8388608 | tf_op jit(solution)/shard_map/all_to_all | solution.py:117
  450.9 21.4 %fusion.46 = f32[1,128,2048]{2,0,1:T(1,128)S(1)} fusion(f32[256,1,2048]{2,0,1:T(8,128)S(1)} %bitcast.128, f32[1,383,2048]{2,1,0:T(8,128)S(1)} %copy-done.19), kind=kOutput, calls=%fused_computation.96 | convolution fusion | flops 805306368 | bytes 6283264 | tf_op jit(solution)/shard_map/conv_general_dilated | solution.py:19
  472.7 5.2 rev.16
  477.9 9.9 %all_gather.3 = f32[8,2048]{1,0:T(8,128)S(1)} all-gather(f32[8,256]{1,0:T(8,128)S(1)} %get-tuple-element.201), channel_id=1, replica_groups=mesh['ctx'=8,'tp'=4] {'ctx'}, dimensions={1}, use_global_device_ids=true | all-gather | bytes 73728 | tf_op jit(solution)/shard_map/all_gather | solution.py:122
  488.4 47.4 %all-reduce.20.cloned.1.call-done = f32[128,2048]{1,0:T(8,128)} async-done(((f32[128,2048]{1,0:T(8,128)}), f32[128,2048]{1,0:T(8,128)}) %all-reduce.20.cloned.1.call-update) | async-done | bytes 1048592 | tf_op jit(solution)/shard_map/psum | solution.py:133
  539.7 21.8 %fusion.38 = f32[1,256,2048]{2,0,1:T(1,128)S(1)} fusion(f32[1,383,2048]{2,1,0:T(8,128)S(1)} %maximum_bitcast_fusion, f32[128,1,2048]{2,0,1:T(8,128)S(1)} %bitcast.139), kind=kOutput, calls=%fused_computation.81 | convolution fusion | flops 805306368 | bytes 6283264 | tf_op jit(solution)/shard_map/conv_general_dilated | solution.py:19
  (758 shorter events, 220.5 us)
Async XLA Ops:
  7.2 61.6 %copy-start = (f32[8,2048]{1,0:T(8,128)S(1)}, f32[8,2048]{1,0:T(8,128)}, u32[]{:S(2)}) copy-start(f32[8,2048]{1,0:T(8,128)} %param.19) | copy-start | bytes 196612
  7.2 20.7 %copy-start.9 = (bf16[256,2048]{1,0:T(8,128)(2,1)S(1)}, bf16[256,2048]{1,0:T(8,128)(2,1)}, u32[]{:S(2)}) copy-start(bf16[256,2048]{1,0:T(8,128)(2,1)} %param.12) | copy-start | bytes 3145732
  7.2 20.7 %copy-start.11 = (bf16[256,2048]{1,0:T(8,128)(2,1)S(1)}, bf16[256,2048]{1,0:T(8,128)(2,1)}, u32[]{:S(2)}) copy-start(bf16[256,2048]{1,0:T(8,128)(2,1)} %param.13) | copy-start | bytes 3145732
  9.3 18.5 %collective-permute-start = (bf16[127,2048]{1,0:T(8,128)(2,1)}, bf16[127,2048]{1,0:T(8,128)(2,1)S(1)}, u32[]{:S(2)}, u32[]{:S(2)}) collective-permute-start(bf16[127,2048]{1,0:T(8,128)(2,1)} %slice.393), channel_id=1, source_target_pairs={{0,4},{4,8},{8,12},{12,16},{16,20},{20,24},{24,28},{1,5},{5,9},{9,... | collective-permute-start | bytes 1560584 | tf_op jit(solution)/shard_map/ppermute | solution.py:14
  13.7 14.1 %collective-permute-start.1 = (bf16[127,2048]{1,0:T(8,128)(2,1)}, bf16[127,2048]{1,0:T(8,128)(2,1)}, u32[]{:S(2)}, u32[]{:S(2)}) collective-permute-start(bf16[127,2048]{1,0:T(8,128)(2,1)} %slice.394), channel_id=1, source_target_pairs={{0,4},{4,8},{8,12},{12,16},{16,20},{20,24},{24,28},{1,5},{5,9},{9,... | collective-permute-start | bytes 1560584 | tf_op jit(solution)/shard_map/ppermute | solution.py:14
  31.3 21.6 %copy-start.13 = (bf16[256,2048]{1,0:T(8,128)(2,1)S(1)}, bf16[256,2048]{1,0:T(8,128)(2,1)}, u32[]{:S(2)}) copy-start(bf16[256,2048]{1,0:T(8,128)(2,1)} %param.15) | copy-start | bytes 3145732
  31.3 21.6 %copy-start.14 = (bf16[256,2048]{1,0:T(8,128)(2,1)S(1)}, bf16[256,2048]{1,0:T(8,128)(2,1)}, u32[]{:S(2)}) copy-start(bf16[256,2048]{1,0:T(8,128)(2,1)} %param.11) | copy-start | bytes 3145732
  31.3 21.6 %copy-start.16 = (bf16[256,2048]{1,0:T(8,128)(2,1)S(1)}, bf16[256,2048]{1,0:T(8,128)(2,1)}, u32[]{:S(2)}) copy-start(bf16[256,2048]{1,0:T(8,128)(2,1)} %param.16) | copy-start | bytes 3145732
  31.3 21.6 %copy-start.20 = (bf16[256,2048]{1,0:T(8,128)(2,1)S(1)}, bf16[256,2048]{1,0:T(8,128)(2,1)}, u32[]{:S(2)}) copy-start(bf16[256,2048]{1,0:T(8,128)(2,1)} %param.14) | copy-start | bytes 3145732
  64.1 53.7 %all-to-all-start = ((f32[2,256,2048]{1,0,2:T(2,128)}), f32[2,256,2048]{1,0,2:T(2,128)}, u32[]{:S(2)}, u32[]{:S(2)}) async-start(f32[2,256,2048]{1,0,2:T(2,128)} %copy.48), calls=%async_computation | async-start | bytes 8388608 | tf_op jit(solution)/shard_map/all_to_all | solution.py:107
  68.7 467.2 %all-reduce.20.cloned.1.call-start = ((), (), s32[]{:S(2)}) async-start(), calls=%async_computation.2 | async-start | bytes 2097152 | tf_op jit(solution)/shard_map/psum | solution.py:133
  131.9 6.1 %copy-start.23 = (f32[8]{0:T(128)S(1)}, f32[8]{0:T(128)}, u32[]{:S(2)}) copy-start(f32[8]{0:T(128)} %param.18) | copy-start | bytes 100
  191.0 6.2 %copy-start.3 = (f32[2048,256]{1,0:T(8,128)S(1)}, f32[2048,256]{1,0:T(8,128)}, u32[]{:S(2)}) copy-start(f32[2048,256]{1,0:T(8,128)} %copy-done.2) | copy-start | bytes 6291460 | tf_op jit(solution)/shard_map/while
  221.3 6.2 %copy-start.3 = (f32[2048,256]{1,0:T(8,128)S(1)}, f32[2048,256]{1,0:T(8,128)}, u32[]{:S(2)}) copy-start(f32[2048,256]{1,0:T(8,128)} %copy-done.2) | copy-start | bytes 6291460 | tf_op jit(solution)/shard_map/while
  251.5 6.2 %copy-start.3 = (f32[2048,256]{1,0:T(8,128)S(1)}, f32[2048,256]{1,0:T(8,128)}, u32[]{:S(2)}) copy-start(f32[2048,256]{1,0:T(8,128)} %copy-done.2) | copy-start | bytes 6291460 | tf_op jit(solution)/shard_map/while
  281.8 6.2 %copy-start.3 = (f32[2048,256]{1,0:T(8,128)S(1)}, f32[2048,256]{1,0:T(8,128)}, u32[]{:S(2)}) copy-start(f32[2048,256]{1,0:T(8,128)} %copy-done.2) | copy-start | bytes 6291460 | tf_op jit(solution)/shard_map/while
  312.0 6.2 %copy-start.3 = (f32[2048,256]{1,0:T(8,128)S(1)}, f32[2048,256]{1,0:T(8,128)}, u32[]{:S(2)}) copy-start(f32[2048,256]{1,0:T(8,128)} %copy-done.2) | copy-start | bytes 6291460 | tf_op jit(solution)/shard_map/while
  342.3 6.2 %copy-start.3 = (f32[2048,256]{1,0:T(8,128)S(1)}, f32[2048,256]{1,0:T(8,128)}, u32[]{:S(2)}) copy-start(f32[2048,256]{1,0:T(8,128)} %copy-done.2) | copy-start | bytes 6291460 | tf_op jit(solution)/shard_map/while
  372.6 6.2 %copy-start.3 = (f32[2048,256]{1,0:T(8,128)S(1)}, f32[2048,256]{1,0:T(8,128)}, u32[]{:S(2)}) copy-start(f32[2048,256]{1,0:T(8,128)} %copy-done.2) | copy-start | bytes 6291460 | tf_op jit(solution)/shard_map/while
  445.1 5.8 %copy-start.19 = (f32[1,383,2048]{2,1,0:T(8,128)S(1)}, f32[1,383,2048]{2,1,0:T(8,128)}, u32[]{:S(2)}) copy-start(f32[1,383,2048]{2,1,0:T(8,128)} %copy-done.18) | copy-start | bytes 9412612
  449.6 88.5 %collective-permute-start.2 = (f32[127,2048]{1,0:T(8,128)}, f32[127,2048]{1,0:T(8,128)}, u32[]{:S(2)}, u32[]{:S(2)}) collective-permute-start(f32[127,2048]{1,0:T(8,128)} %slice.517), channel_id=1, source_target_pairs={{4,0},{8,4},{12,8},{16,12},{20,16},{24,20},{28,24},{5,1},{9,5},{13... | collective-permute-start | bytes 3121160 | tf_op jit(solution)/shard_map/ppermute | solution.py:14
  539.7 21.8 %copy-start.10 = (bf16[256,2048]{1,0:T(8,128)(2,1)S(1)}, bf16[256,2048]{1,0:T(8,128)(2,1)}, u32[]{:S(2)}) copy-start(bf16[256,2048]{1,0:T(8,128)(2,1)} %param.12) | copy-start | bytes 3145732
  539.7 21.8 %copy-start.12 = (bf16[256,2048]{1,0:T(8,128)(2,1)S(1)}, bf16[256,2048]{1,0:T(8,128)(2,1)}, u32[]{:S(2)}) copy-start(bf16[256,2048]{1,0:T(8,128)(2,1)} %param.13) | copy-start | bytes 3145732
  539.7 24.3 %copy-start.1 = (f32[8,2048]{1,0:T(8,128)S(1)}, f32[8,2048]{1,0:T(8,128)}, u32[]{:S(2)}) copy-start(f32[8,2048]{1,0:T(8,128)} %param.19) | copy-start | bytes 196612
  (33 other events, 76.4 us)
Sparse Core Ops, SparseCore 0:
  478.0 57.7 all-reduce.19
where the time goes:
time: 574 us; the launch traced here: 571 us
  local copies, waits for them, and re-layouts  134 us (23%)
  other arithmetic  128 us (22%)
  matrix products  108 us (19%)
  waiting for transfers between devices  96.4 us (17%)
  blocking collectives  61.4 us (11%)
  between operations  14.4 us (3%)
  loops' own time  13.9 us (2%)
  starting transfers between devices  13.6 us (2%)
    conv_general_dilated x3, matrix products, depthwise(): lax.conv_general_dilated(signal[None], kernel[:, None, :], (1,), 'VALID',...  64.7 us
    all_to_all x1, blocking collectives, per_device(): lax.all_to_all(jnp.stack([conv_seq, back_seq]), 'ctx', split_axis=1, conc...  51.5 us
    all_to_all x1, waiting for transfers between devices, per_device(): lax.all_to_all(jnp.stack([li_input, li_cotan]), 'ctx', split_axis=2, conc...  49 us
    add x8, other arithmetic, one_mode(): back_sum = back_sum + residue_row[None, :] * reverse_states  48.2 us
    psum x1, waiting for transfers between devices, per_device(): tap_sum = lax.psum(tap_part, 'ctx')  47.4 us
    reduce_sum x8, other arithmetic, one_mode(): jnp.sum(inputs * reverse_states, 0)  32.1 us
    dot_general x8, matrix products, one_mode(): backward = jnp.einsum('jt,bjc->btc', toeplitz, co_blocks, precision=highest)  27.8 us
    add x8, other arithmetic, one_mode(): forward + lead_pows[None, :, None] * forward_in[:, None, :]  26.2 us
  transfers between devices with their start and end apart: 5, of which 2 were waited for; matrix products, arithmetic and copies ran while one was open for 7% of the time, Pallas kernels for 0%

commit v1 on v0

--- a/solution.py
+++ b/solution.py
@@ -6,6 +6,17 @@
 
 BLOCK = 128
 highest = lax.Precision.HIGHEST
+
+
+def split_up(value, dim, count):
+    before, after = (value.shape[:dim], value.shape[dim + 1 :])
+    return jnp.moveaxis(value.reshape(*before, count, -1, *after), dim, 0)
+
+
+def joined_along(blocks, dim):
+    blocks = jnp.moveaxis(blocks, 0, dim)
+    lengths = blocks.shape
+    return blocks.reshape(*lengths[:dim], lengths[dim] * lengths[dim + 1], *lengths[dim + 2 :])
 
 
 def from_behind(value, axis, by):
@@ -104,9 +115,15 @@
     cotan = cotangent.astype(jnp.float32)
     li_input = key_second * mr_out
     li_cotan = cotan * query_li.astype(jnp.float32)
-    regrouped = lax.all_to_all(
-        jnp.stack([li_input, li_cotan]), "ctx", split_axis=2, concat_axis=1, tiled=True
-    )
+    x = jnp.stack([li_input, li_cotan])
+    size_2, index = (lax.axis_size("ctx"), lax.axis_index("ctx"))
+    blocks_2 = split_up(x, 2, size_2)
+    gathered = [blocks_2[index]]
+    for step in range(1, size_2):
+        sent = blocks_2[index ^ step]
+        gathered.append(lax.ppermute(sent, "ctx", [(i_2, i_2 ^ step) for i_2 in range(size_2)]))
+    blocks_2 = jnp.stack(gathered)[index ^ jnp.arange(size_2)]
+    regrouped = joined_along(blocks_2, 1)
     piece_cols = channels // devices_ctx
     local_residues = lax.dynamic_slice_in_dim(
         residues, lax.axis_index("ctx") * piece_cols, piece_cols, 1

time: 574 us -> 560 us (0.976)
  waiting for transfers between devices: 96.4 us -> 84 us
    all_to_all x1 -> x0, waiting for transfers between devices: 49 us -> none  [per_device(): lax.all_to_all(jnp.stack([li_input, li_cotan]), 'ctx', split_axis=2, conc...]
    ppermute x0 -> x7, waiting for transfers between devices: none -> 36.6 us  [per_device(): lax.ppermute(sent, 'ctx', [(i_2, i_2 ^ step) for i_2 in range(size_2)])]
    unnamed x43 -> x60, local copies, waits for them, and re-layouts: 5.08 us -> 18.7 us
    slice x2 -> x1, local copies, waits for them, and re-layouts: 15.6 us -> 4.01 us  [per_device(): regrouped[1]]
    ppermute x0 -> x7, starting transfers between devices: none -> 9.39 us  [per_device(): lax.ppermute(sent, 'ctx', [(i_2, i_2 ^ step) for i_2 in range(size_2)])]
  transfers between devices with their start and end apart: 5 -> 11, of which waited for: 2 -> 4; matrix products, arithmetic and copies ran while one was open for 7% -> 9% of each run, Pallas kernels for 0% -> 0%
where the time goes in v1:
time: 560 us; the launch traced here: 558 us
  local copies, waits for them, and re-layouts  131 us (23%)
  other arithmetic  126 us (22%)
  matrix products  108 us (19%)
  waiting for transfers between devices  84 us (15%)
  blocking collectives  61.6 us (11%)
  starting transfers between devices  18.4 us (3%)
  between operations  14.5 us (3%)
  loops' own time  14 us (2%)
    conv_general_dilated x3, matrix products, depthwise(): lax.conv_general_dilated(signal[None], kernel[:, None, :], (1,), 'VALID',...  64.7 us
    all_to_all x1, blocking collectives, per_device(): lax.all_to_all(jnp.stack([conv_seq, back_seq]), 'ctx', split_axis=1, conc...  51.7 us
    add x8, other arithmetic, one_mode(): back_sum = back_sum + residue_row[None, :] * reverse_states  48.2 us
    psum x1, waiting for transfers between devices, per_device(): tap_sum = lax.psum(tap_part, 'ctx')  47.4 us
    ppermute x7, waiting for transfers between devices, per_device(): lax.ppermute(sent, 'ctx', [(i_2, i_2 ^ step) for i_2 in range(size_2)])  36.6 us
    reduce_sum x8, other arithmetic, one_mode(): jnp.sum(inputs * reverse_states, 0)  32 us
    dot_general x8, matrix products, one_mode(): backward = jnp.einsum('jt,bjc->btc', toeplitz, co_blocks, precision=highest)  27.8 us
    add x8, other arithmetic, one_mode(): forward + lead_pows[None, :, None] * forward_in[:, None, :]  26.1 us
  transfers between devices with their start and end apart: 11, of which 4 were waited for; matrix products, arithmetic and copies ran while one was open for 9% of the time, Pallas kernels for 0%

profile of v1, /device:TPU:0, one launch (start us, length us, event | category | flops | bytes accessed | tf_op | source)
XLA Modules:
  0.0 557.7 jit_solution(15480097392421304041)
XLA Ops:
  14.5 4.5 collective-permute-start.1
  19.1 5.2 rev.15
  28.1 21.5 %fusion.47 = f32[1,256,2048]{2,0,1:T(1,128)S(1)} fusion(f32[1,383,2048]{2,1,0:T(8,128)S(1)} %convert_multiply_fusion, f32[128,1,2048]{2,0,1:T(8,128)S(1)} %bitcast.188), kind=kOutput, calls=%fused_computation.100 | convolution fusion | flops 805306368 | bytes 6283264 | tf_op jit(solution)/shard_map/conv_general_dilated | solution.py:30
  78.3 7.1 %collective-permute-done.4 = f32[2,256,256]{2,1,0:T(8,128)S(1)} collective-permute-done((f32[2,256,256]{2,1,0:T(8,128)S(1)}, f32[2,256,256]{2,1,0:T(8,128)S(1)}, u32[]{:S(2)}, u32[]{:S(2)}) %collective-permute-start.4) | collective-permute-done | bytes 524320 | tf_op jit(solution)/shard_map/ppermute | solution.py:124
  87.1 26.1 %collective-permute-done.6 = f32[2,256,256]{2,1,0:T(8,128)S(1)} collective-permute-done((f32[2,256,256]{2,1,0:T(8,128)S(1)}, f32[2,256,256]{2,1,0:T(8,128)S(1)}, u32[]{:S(2)}, u32[]{:S(2)}) %collective-permute-start.6) | collective-permute-done | bytes 524320 | tf_op jit(solution)/shard_map/ppermute | solution.py:124
  115.7 5.0 gather_fusion
  120.7 4.0 fusion.57
  124.7 240.8 %while.19 = (s32[]{:T(128)}, f32[2048,256]{1,0:T(8,128)}, f32[2048,256]{1,0:T(8,128)}, f32[8,256]{1,0:T(8,128)S(1)}, f32[8,256]{1,0:T(8,128)S(1)}, /*index=5*/f3...) while((s32[]{:T(128)}, f32[2048,256]{1,0:T(8,128)}, ...), condition=%wide.region_2.3_spmd.clone.clone, body=%wide.region_0.2_spmd.clone.clone.sunk | while | flops 1617155328 | bytes 74435056 | solution.py:90
  142.1 4.0 fusion.88
  148.8 4.9 fusion.89
  177.8 6.2 %fusion.89 = (f32[2048,256]{1,0:T(8,128)}, f32[2048,256]{1,0:T(8,128)}) fusion(f32[16,128,256]{2,1,0:T(8,128)} %copy.121, f32[2048,256]{1,0:T(8,128)} %get-tuple-element.420, f32[256]{0:T(256)S(1)} %bitcast.194, pred[]{:T(512)S(6)} %compare.24, f32[16,128,256]{2,1,0:T(8,128)} %multiply_add_fusion.22, f32[2048,256]{1,0:T(8,128)} %get-tuple-element.419), kind=kLoop, calls=%fused_computation.4.clone.1 | loop fusion | flops 3145728 | bytes 12583937 | tf_op jit(solution)/shard_map/while/body/eval_jaxpr/add | solution.py:80
  208.0 6.2 %fusion.89 = (f32[2048,256]{1,0:T(8,128)}, f32[2048,256]{1,0:T(8,128)}) fusion(f32[16,128,256]{2,1,0:T(8,128)} %copy.121, f32[2048,256]{1,0:T(8,128)} %get-tuple-element.420, f32[256]{0:T(256)S(1)} %bitcast.194, pred[]{:T(512)S(6)} %compare.24, f32[16,128,256]{2,1,0:T(8,128)} %multiply_add_fusion.22, f32[2048,256]{1,0:T(8,128)} %get-tuple-element.419), kind=kLoop, calls=%fused_computation.4.clone.1 | loop fusion | flops 3145728 | bytes 12583937 | tf_op jit(solution)/shard_map/while/body/eval_jaxpr/add | solution.py:80
  238.3 6.2 %fusion.89 = (f32[2048,256]{1,0:T(8,128)}, f32[2048,256]{1,0:T(8,128)}) fusion(f32[16,128,256]{2,1,0:T(8,128)} %copy.121, f32[2048,256]{1,0:T(8,128)} %get-tuple-element.420, f32[256]{0:T(256)S(1)} %bitcast.194, pred[]{:T(512)S(6)} %compare.24, f32[16,128,256]{2,1,0:T(8,128)} %multiply_add_fusion.22, f32[2048,256]{1,0:T(8,128)} %get-tuple-element.419), kind=kLoop, calls=%fused_computation.4.clone.1 | loop fusion | flops 3145728 | bytes 12583937 | tf_op jit(solution)/shard_map/while/body/eval_jaxpr/add | solution.py:80
  268.6 6.2 %fusion.89 = (f32[2048,256]{1,0:T(8,128)}, f32[2048,256]{1,0:T(8,128)}) fusion(f32[16,128,256]{2,1,0:T(8,128)} %copy.121, f32[2048,256]{1,0:T(8,128)} %get-tuple-element.420, f32[256]{0:T(256)S(1)} %bitcast.194, pred[]{:T(512)S(6)} %compare.24, f32[16,128,256]{2,1,0:T(8,128)} %multiply_add_fusion.22, f32[2048,256]{1,0:T(8,128)} %get-tuple-element.419), kind=kLoop, calls=%fused_computation.4.clone.1 | loop fusion | flops 3145728 | bytes 12583937 | tf_op jit(solution)/shard_map/while/body/eval_jaxpr/add | solution.py:80
  298.8 6.2 %fusion.89 = (f32[2048,256]{1,0:T(8,128)}, f32[2048,256]{1,0:T(8,128)}) fusion(f32[16,128,256]{2,1,0:T(8,128)} %copy.121, f32[2048,256]{1,0:T(8,128)} %get-tuple-element.420, f32[256]{0:T(256)S(1)} %bitcast.194, pred[]{:T(512)S(6)} %compare.24, f32[16,128,256]{2,1,0:T(8,128)} %multiply_add_fusion.22, f32[2048,256]{1,0:T(8,128)} %get-tuple-element.419), kind=kLoop, calls=%fused_computation.4.clone.1 | loop fusion | flops 3145728 | bytes 12583937 | tf_op jit(solution)/shard_map/while/body/eval_jaxpr/add | solution.py:80
  329.1 6.2 %fusion.89 = (f32[2048,256]{1,0:T(8,128)}, f32[2048,256]{1,0:T(8,128)}) fusion(f32[16,128,256]{2,1,0:T(8,128)} %copy.121, f32[2048,256]{1,0:T(8,128)} %get-tuple-element.420, f32[256]{0:T(256)S(1)} %bitcast.194, pred[]{:T(512)S(6)} %compare.24, f32[16,128,256]{2,1,0:T(8,128)} %multiply_add_fusion.22, f32[2048,256]{1,0:T(8,128)} %get-tuple-element.419), kind=kLoop, calls=%fused_computation.4.clone.1 | loop fusion | flops 3145728 | bytes 12583937 | tf_op jit(solution)/shard_map/while/body/eval_jaxpr/add | solution.py:80
  359.3 6.2 %fusion.89 = (f32[2048,256]{1,0:T(8,128)}, f32[2048,256]{1,0:T(8,128)}) fusion(f32[16,128,256]{2,1,0:T(8,128)} %copy.121, f32[2048,256]{1,0:T(8,128)} %get-tuple-element.420, f32[256]{0:T(256)S(1)} %bitcast.194, pred[]{:T(512)S(6)} %compare.24, f32[16,128,256]{2,1,0:T(8,128)} %multiply_add_fusion.22, f32[2048,256]{1,0:T(8,128)} %get-tuple-element.419), kind=kLoop, calls=%fused_computation.4.clone.1 | loop fusion | flops 3145728 | bytes 12583937 | tf_op jit(solution)/shard_map/while/body/eval_jaxpr/add | solution.py:80
  370.5 4.1 pad_maximum_fusion.6
  374.6 51.7 %all_to_all.15 = f32[2,2048,256]{2,0,1:T(2,128)S(1)} all-to-all(f32[2,2048,256]{2,0,1:T(2,128)S(1)} %pad_maximum_fusion.6), channel_id=1, replica_groups=mesh['ctx'=8,'tp'=4] {'ctx'}, dimensions={1} | all-to-all | bytes 8388608 | tf_op jit(solution)/shard_map/all_to_all | solution.py:134
  437.8 21.4 %fusion.44 = f32[1,128,2048]{2,0,1:T(1,128)S(1)} fusion(f32[256,1,2048]{2,0,1:T(8,128)S(1)} %bitcast.172, f32[1,383,2048]{2,1,0:T(8,128)S(1)} %copy-done.18), kind=kOutput, calls=%fused_computation.96 | convolution fusion | flops 805306368 | bytes 6283264 | tf_op jit(solution)/shard_map/conv_general_dilated | solution.py:30
  459.5 5.2 rev.16
  464.7 9.9 %all_gather.3 = f32[8,2048]{1,0:T(8,128)S(1)} all-gather(f32[8,256]{1,0:T(8,128)S(1)} %get-tuple-element.201), channel_id=1, replica_groups=mesh['ctx'=8,'tp'=4] {'ctx'}, dimensions={1}, use_global_device_ids=true | all-gather | bytes 73728 | tf_op jit(solution)/shard_map/all_gather | solution.py:139
  475.2 47.4 %all-reduce.20.cloned.1.call-done = f32[128,2048]{1,0:T(8,128)} async-done(((f32[128,2048]{1,0:T(8,128)}), f32[128,2048]{1,0:T(8,128)}) %all-reduce.20.cloned.1.call-update) | async-done | bytes 1048592 | tf_op jit(solution)/shard_map/psum | solution.py:150
  526.6 21.8 %fusion.38 = f32[1,256,2048]{2,0,1:T(1,128)S(1)} fusion(f32[1,383,2048]{2,1,0:T(8,128)S(1)} %maximum_bitcast_fusion, f32[128,1,2048]{2,0,1:T(8,128)S(1)} %bitcast.187), kind=kOutput, calls=%fused_computation.81 | convolution fusion | flops 805306368 | bytes 6283264 | tf_op jit(solution)/shard_map/conv_general_dilated | solution.py:30
  (790 shorter events, 242.1 us)
Async XLA Ops:
  7.2 50.2 %copy-start = (f32[8,2048]{1,0:T(8,128)S(1)}, f32[8,2048]{1,0:T(8,128)}, u32[]{:S(2)}) copy-start(f32[8,2048]{1,0:T(8,128)} %param.19) | copy-start | bytes 196612
  7.2 11.9 %copy-start.19 = (f32[128,2048]{1,0:T(8,128)S(1)}, f32[128,2048]{1,0:T(8,128)}, u32[]{:S(2)}) copy-start(f32[128,2048]{1,0:T(8,128)} %param.17) | copy-start | bytes 3145732
  7.2 17.1 %copy-start.22 = (bf16[256,2048]{1,0:T(8,128)(2,1)S(1)}, bf16[256,2048]{1,0:T(8,128)(2,1)}, u32[]{:S(2)}) copy-start(bf16[256,2048]{1,0:T(8,128)(2,1)} %param.14) | copy-start | bytes 3145732
  7.2 17.0 %copy-start.15 = (bf16[256,2048]{1,0:T(8,128)(2,1)S(1)}, bf16[256,2048]{1,0:T(8,128)(2,1)}, u32[]{:S(2)}) copy-start(bf16[256,2048]{1,0:T(8,128)(2,1)} %param.16) | copy-start | bytes 3145732
  7.2 515.4 %all-reduce.20.cloned.1.call-start = ((), (), s32[]{:S(2)}) async-start(), calls=%async_computation.1 | async-start | bytes 2097152 | tf_op jit(solution)/shard_map/psum | solution.py:150
  9.4 16.2 %collective-permute-start = (bf16[127,2048]{1,0:T(8,128)(2,1)}, bf16[127,2048]{1,0:T(8,128)(2,1)}, u32[]{:S(2)}, u32[]{:S(2)}) collective-permute-start(bf16[127,2048]{1,0:T(8,128)(2,1)} %slice.393), channel_id=1, source_target_pairs={{0,4},{4,8},{8,12},{12,16},{16,20},{20,24},{24,28},{1,5},{5,9},{9,... | collective-permute-start | bytes 1560584 | tf_op jit(solution)/shard_map/ppermute | solution.py:25
  14.5 11.0 %collective-permute-start.1 = (bf16[127,2048]{1,0:T(8,128)(2,1)}, bf16[127,2048]{1,0:T(8,128)(2,1)}, u32[]{:S(2)}, u32[]{:S(2)}) collective-permute-start(bf16[127,2048]{1,0:T(8,128)(2,1)} %slice.394), channel_id=1, source_target_pairs={{0,4},{4,8},{8,12},{12,16},{16,20},{20,24},{24,28},{1,5},{5,9},{9,... | collective-permute-start | bytes 1560584 | tf_op jit(solution)/shard_map/ppermute | solution.py:25
  28.1 21.6 %copy-start.17 = (f32[1,383,2048]{2,1,0:T(8,128)}, f32[1,383,2048]{2,1,0:T(8,128)S(1)}, u32[]{:S(2)}) copy-start(f32[1,383,2048]{2,1,0:T(8,128)S(1)} %convert_multiply_fusion) | copy-start | bytes 9412612
  28.1 21.6 %copy-start.12 = (bf16[256,2048]{1,0:T(8,128)(2,1)S(1)}, bf16[256,2048]{1,0:T(8,128)(2,1)}, u32[]{:S(2)}) copy-start(bf16[256,2048]{1,0:T(8,128)(2,1)} %param.15) | copy-start | bytes 3145732
  28.1 21.6 %copy-start.13 = (bf16[256,2048]{1,0:T(8,128)(2,1)S(1)}, bf16[256,2048]{1,0:T(8,128)(2,1)}, u32[]{:S(2)}) copy-start(bf16[256,2048]{1,0:T(8,128)(2,1)} %param.11) | copy-start | bytes 3145732
  56.8 10.9 %collective-permute-start.2 = (f32[2,256,256]{2,1,0:T(8,128)}, f32[2,256,256]{2,1,0:T(8,128)}, u32[]{:S(2)}, u32[]{:S(2)}) collective-permute-start(f32[2,256,256]{2,1,0:T(8,128)} %bitcast.126), channel_id=1, source_target_pairs={{0,4},{4,0},{8,12},{12,8},{16,20},{20,16},{24,28},{28,24},{1,5},{5... | collective-permute-start | bytes 1572872 | tf_op jit(solution)/shard_map/ppermute | solution.py:124
  59.2 15.5 %collective-permute-start.3 = (f32[2,256,256]{2,1,0:T(8,128)}, f32[2,256,256]{2,1,0:T(8,128)}, u32[]{:S(2)}, u32[]{:S(2)}) collective-permute-start(f32[2,256,256]{2,1,0:T(8,128)} %bitcast.125), channel_id=1, source_target_pairs={{0,8},{4,12},{8,0},{12,4},{16,24},{20,28},{24,16},{28,20},{1,9},{5... | collective-permute-start | bytes 1572872 | tf_op jit(solution)/shard_map/ppermute | solution.py:124
  62.7 22.7 %collective-permute-start.4 = (f32[2,256,256]{2,1,0:T(8,128)S(1)}, f32[2,256,256]{2,1,0:T(8,128)S(1)}, u32[]{:S(2)}, u32[]{:S(2)}) collective-permute-start(f32[2,256,256]{2,1,0:T(8,128)S(1)} %bitcast.191), channel_id=1, source_target_pairs={{0,12},{4,8},{8,4},{12,0},{16,28},{20,24},{24,20},{28,16},{1,13},{... | collective-permute-start | bytes 1572872 | tf_op jit(solution)/shard_map/ppermute | solution.py:124
  64.8 21.5 %collective-permute-start.5 = (f32[2,256,256]{2,1,0:T(8,128)S(1)}, f32[2,256,256]{2,1,0:T(8,128)S(1)}, u32[]{:S(2)}, u32[]{:S(2)}) collective-permute-start(f32[2,256,256]{2,1,0:T(8,128)S(1)} %bitcast.193), channel_id=1, source_target_pairs={{0,16},{4,20},{8,24},{12,28},{16,0},{20,4},{24,8},{28,12},{1,17},{... | collective-permute-start | bytes 1572872 | tf_op jit(solution)/shard_map/ppermute | solution.py:124
  67.5 45.7 %collective-permute-start.6 = (f32[2,256,256]{2,1,0:T(8,128)S(1)}, f32[2,256,256]{2,1,0:T(8,128)S(1)}, u32[]{:S(2)}, u32[]{:S(2)}) collective-permute-start(f32[2,256,256]{2,1,0:T(8,128)S(1)} %bitcast.192), channel_id=1, source_target_pairs={{0,20},{4,16},{8,28},{12,24},{16,4},{20,0},{24,12},{28,8},{1,21},{... | collective-permute-start | bytes 1572872 | tf_op jit(solution)/shard_map/ppermute | solution.py:124
  67.7 46.3 %collective-permute-start.7 = (f32[2,256,256]{2,1,0:T(8,128)S(1)}, f32[2,256,256]{2,1,0:T(8,128)S(1)}, u32[]{:S(2)}, u32[]{:S(2)}) collective-permute-start(f32[2,256,256]{2,1,0:T(8,128)S(1)} %bitcast.190), channel_id=1, source_target_pairs={{0,24},{4,28},{8,16},{12,20},{16,8},{20,12},{24,0},{28,4},{1,25},{... | collective-permute-start | bytes 1572872 | tf_op jit(solution)/shard_map/ppermute | solution.py:124
  74.7 40.2 %collective-permute-start.8 = (f32[2,256,256]{2,1,0:T(8,128)S(1)}, f32[2,256,256]{2,1,0:T(8,128)S(1)}, u32[]{:S(2)}, u32[]{:S(2)}) collective-permute-start(f32[2,256,256]{2,1,0:T(8,128)S(1)} %bitcast.189), channel_id=1, source_target_pairs={{0,28},{4,24},{8,20},{12,16},{16,12},{20,8},{24,4},{28,0},{1,29},{... | collective-permute-start | bytes 1572872 | tf_op jit(solution)/shard_map/ppermute | solution.py:124
  177.8 6.2 %copy-start.3 = (f32[2048,256]{1,0:T(8,128)S(1)}, f32[2048,256]{1,0:T(8,128)}, u32[]{:S(2)}) copy-start(f32[2048,256]{1,0:T(8,128)} %copy-done.2) | copy-start | bytes 6291460 | tf_op jit(solution)/shard_map/while
  268.6 6.2 %copy-start.3 = (f32[2048,256]{1,0:T(8,128)S(1)}, f32[2048,256]{1,0:T(8,128)}, u32[]{:S(2)}) copy-start(f32[2048,256]{1,0:T(8,128)} %copy-done.2) | copy-start | bytes 6291460 | tf_op jit(solution)/shard_map/while
  329.1 6.2 %copy-start.3 = (f32[2048,256]{1,0:T(8,128)S(1)}, f32[2048,256]{1,0:T(8,128)}, u32[]{:S(2)}) copy-start(f32[2048,256]{1,0:T(8,128)} %copy-done.2) | copy-start | bytes 6291460 | tf_op jit(solution)/shard_map/while
  436.5 88.5 %collective-permute-start.9 = (f32[127,2048]{1,0:T(8,128)}, f32[127,2048]{1,0:T(8,128)}, u32[]{:S(2)}, u32[]{:S(2)}) collective-permute-start(f32[127,2048]{1,0:T(8,128)} %slice.519), channel_id=1, source_target_pairs={{4,0},{8,4},{12,8},{16,12},{20,16},{24,20},{28,24},{5,1},{9,5},{13... | collective-permute-start | bytes 3121160 | tf_op jit(solution)/shard_map/ppermute | solution.py:25
  526.5 21.8 %copy-start.10 = (bf16[256,2048]{1,0:T(8,128)(2,1)S(1)}, bf16[256,2048]{1,0:T(8,128)(2,1)}, u32[]{:S(2)}) copy-start(bf16[256,2048]{1,0:T(8,128)(2,1)} %param.12) | copy-start | bytes 3145732
  526.6 21.8 %copy-start.11 = (bf16[256,2048]{1,0:T(8,128)(2,1)S(1)}, bf16[256,2048]{1,0:T(8,128)(2,1)}, u32[]{:S(2)}) copy-start(bf16[256,2048]{1,0:T(8,128)(2,1)} %param.13) | copy-start | bytes 3145732
  526.6 24.3 %copy-start.1 = (f32[8,2048]{1,0:T(8,128)S(1)}, f32[8,2048]{1,0:T(8,128)}, u32[]{:S(2)}) copy-start(f32[8,2048]{1,0:T(8,128)} %param.19) | copy-start | bytes 196612
  (39 other events, 109.5 us)
Sparse Core Ops, SparseCore 0:
  464.8 57.7 all-reduce.19
